TPU v7x, 128 devices: a whole 4x4x4 slice. The times are simulated.
128 devices in a mesh: pipe: 2 (over x_hi), tensor: 4 (over z), dp: 16 (over x_lo, y, core).
Axes of the slice: x: 4 (x_hi: 2, x_lo: 2; x = x_hi * 2 + x_lo), y: 4, z: 4, core: 2. Of those that a mesh axis runs over, the one named last changes fastest.
Arguments:
- tokens: bfloat16 [8192, 1024], P('dp', 'tensor'), may hold values from -6 to 6
- lengths: int32 [64, 4], P('dp'), may hold values from 1 to 85, 128 in all within a row
- ln_gain: bfloat16 [2, 2, 1024], P('pipe'), may hold values from 0.099609375 to 1.8984375
- ln_bias: bfloat16 [2, 2, 1024], P('pipe'), may hold values from -3 to 3
- joined_weight: bfloat16 [2, 1024, 3, 1024], P('pipe', None, None, 'tensor'), may hold values from -0.1875 to 0.1875
- joined_bias: bfloat16 [2, 3, 1024], P('pipe', None, 'tensor'), may hold values from -3 to 3
- dense_weight: bfloat16 [2, 1024, 1024], P('pipe', 'tensor'), may hold values from -0.5 to 0.5
- up_weight: bfloat16 [2, 1024, 4096], P('pipe', None, 'tensor'), may hold values from -0.1875 to 0.1875
- up_bias: bfloat16 [2, 4096], P('pipe', 'tensor'), may hold values from -3 to 3
- down_weight: bfloat16 [2, 4096, 1024], P('pipe', 'tensor'), may hold values from -0.09375 to 0.09375
- output_bias: bfloat16 [2, 2, 1024], P('pipe'), may hold values from -3 to 3
- cotangent: bfloat16 [8192, 1024], P('dp', 'tensor'), may hold values from -6 to 6
Outputs:
- section_out: bfloat16 [2, 8192, 1024], P('pipe', 'dp', 'tensor')
- input_grad: bfloat16 [2, 8192, 1024], P('pipe', 'dp', 'tensor')
- grad_ln_gain: float32 [2, 2, 1024], P('pipe')
- grad_ln_bias: float32 [2, 2, 1024], P('pipe')
- grad_joined: float32 [2, 1024, 3, 1024], P('pipe', None, None, 'tensor')
- grad_joined_bias: float32 [2, 3, 1024], P('pipe', None, 'tensor')
- grad_dense: float32 [2, 1024, 1024], P('pipe', 'tensor')
- grad_up: float32 [2, 1024, 4096], P('pipe', None, 'tensor')
- grad_up_bias: float32 [2, 4096], P('pipe', 'tensor')
- grad_down: float32 [2, 4096, 1024], P('pipe', 'tensor')
- grad_output_bias: float32 [2, 2, 1024], P('pipe')
Inputs may be any that keep to these rules, and one draw needn't show every extreme that they name: Row b gives, in order, the lengths of the 4 sequences that fill block b (tokens b * 128 to (b + 1) * 128 - 1); every row sums to 128.
All inputs are finite; a program needn't handle non-finite values.
Results may differ from a plain program's by a relative error of at most 0.035.
Values may be sent and summed in bfloat16 or wider, within the bound.
No kernel may reach another device: no remote copies, remote signals or barrier semaphores. Data moves between devices by JAX's collectives and lax.ppermute only.
A program may use at most 192 MiB of HBM per device.

v0:
```python
import jax
import jax.numpy as jnp
from jax import lax
from jax.sharding import PartitionSpec as P

HD = 64
ROT = 16
MB = 128
NMB = 4
EPSILON = 1e-05
MASKED = -1e30


def passed_along(x, axis, by):
    peers = lax.axis_size(axis)
    pairs = [(i, i + by) for i in range(peers) if 0 <= i + by < peers]
    return lax.ppermute(x, axis, pairs)


def as_sent(x):
    return jax.tree.map(lambda a: a.astype(jnp.bfloat16) if a.dtype == jnp.float32 else a, x)


def positions(lengths, block_rows):
    seq_count = lengths.shape[1]
    counter = jnp.arange(seq_count, dtype=jnp.int32)
    lower_tri = (counter[:, None] >= counter[None, :]).astype(jnp.int32)
    seg_ends = jnp.sum(lengths[:, None, :] * lower_tri[None, :, :], axis=2)
    starts = seg_ends - lengths
    row_index = jnp.arange(block_rows, dtype=jnp.int32)
    segment = jnp.sum((row_index[None, :, None] >= seg_ends[:, None, :]).astype(jnp.int32), axis=2)
    member = (segment[:, :, None] == counter[None, None, :]).astype(jnp.int32)
    place = row_index[None, :] - jnp.sum(member * starts[:, None, :], axis=2)
    return (segment, place)


def rotary(place):
    half_rot = ROT // 2
    inv_freq = jnp.power(10000.0, -2.0 * jnp.arange(half_rot, dtype=jnp.float32) / ROT)
    angles = place.astype(jnp.float32)[..., None] * inv_freq
    return (jnp.cos(angles), jnp.sin(angles))


def rotate(heads_in, cosv, sinv):
    half_rot = ROT // 2
    first_half = heads_in[..., :half_rot]
    second_half = heads_in[..., half_rot:ROT]
    cos_rows = cosv[:, None, :]
    sin_rows = sinv[:, None, :]
    return jnp.concatenate(
        [
            first_half * cos_rows - second_half * sin_rows,
            second_half * cos_rows + first_half * sin_rows,
            heads_in[..., ROT:],
        ],
        axis=-1,
    )


def rotate_back(heads_in, cosv, sinv):
    half_rot = ROT // 2
    first_half = heads_in[..., :half_rot]
    second_half = heads_in[..., half_rot:ROT]
    cos_rows = cosv[:, None, :]
    sin_rows = sinv[:, None, :]
    return jnp.concatenate(
        [
            first_half * cos_rows + second_half * sin_rows,
            second_half * cos_rows - first_half * sin_rows,
            heads_in[..., ROT:],
        ],
        axis=-1,
    )


def exact_gelu(values):
    return jax.nn.gelu(values, approximate=False)


def allowed_keys(segment):
    row_index = jnp.arange(segment.shape[0], dtype=jnp.int32)
    return (segment[:, None] == segment[None, :]) & (row_index[None, :] <= row_index[:, None])


def contract_rows(left, right):
    return lax.dot_general(
        left, right, (((0,), (0,)), ((), ())), preferred_element_type=jnp.float32
    )


def contract_cols(left, right):
    return lax.dot_general(
        left, right, (((1,), (1,)), ((), ())), preferred_element_type=jnp.float32
    )


def per_device(
    tokens,
    lengths,
    ln_gain,
    ln_bias,
    joined_weight,
    joined_bias,
    dense_weight,
    up_weight,
    up_bias,
    down_weight,
    output_bias,
    cotangent,
):
    leading = lax.axis_index("pipe") == 0
    model_width = joined_weight.shape[1]
    local_width = joined_weight.shape[3]
    local_heads = local_width // HD
    hidden_local = up_weight.shape[2]
    quarter = tokens.shape[1]
    score_scale = HD ** (-0.5)
    ln_gains = ln_gain[0].astype(jnp.float32)
    ln_shifts = ln_bias[0].astype(jnp.float32)
    joined_mat = joined_weight[0].reshape(model_width, 3 * local_width)
    joined_add = joined_bias[0].astype(jnp.float32).reshape(3 * local_width)
    dense_mat = dense_weight[0]
    up_mat = up_weight[0]
    up_add = up_bias[0].astype(jnp.float32)
    down_mat = down_weight[0]
    bias_sum = output_bias[0, 0].astype(jnp.float32) + output_bias[0, 1].astype(jnp.float32)
    input_rows, output_grads = (
        lax.all_gather(tokens, "tensor", axis=1, tiled=True),
        lax.all_gather(cotangent, "tensor", axis=1, tiled=True),
    )
    segment_all, place_all = positions(lengths, MB)
    cos_all, sin_all = rotary(place_all)

    def pick(early_val, late_val):
        return jax.tree.map(
            lambda upper_val, lower_val: jnp.where(leading, upper_val, lower_val),
            early_val,
            late_val,
        )

    received = jnp.zeros((MB, model_width), jnp.bfloat16)
    tick_outputs = []
    tick_stored = []
    for section_tick in range(NMB + 1):
        early_block = min(section_tick, NMB - 1)
        late_block = max(section_tick - 1, 0)
        block_rows = jnp.where(
            leading, input_rows[early_block * MB : (early_block + 1) * MB], received
        )
        segment, cosv, sinv = pick(
            (segment_all[early_block], cos_all[early_block], sin_all[early_block]),
            (segment_all[late_block], cos_all[late_block], sin_all[late_block]),
        )
        inputs = block_rows.astype(jnp.float32)
        row_mean = jnp.mean(inputs, axis=1, keepdims=True)
        centred = inputs - row_mean
        forward_inv_scale = lax.rsqrt(jnp.mean(centred * centred, axis=1, keepdims=True) + EPSILON)
        forward_normed = centred * forward_inv_scale
        forward_h_attn = (forward_normed * ln_gains[0] + ln_shifts[0]).astype(jnp.bfloat16)
        forward_h_mlp = (forward_normed * ln_gains[1] + ln_shifts[1]).astype(jnp.bfloat16)
        joined_proj = (
            jnp.dot(forward_h_attn, joined_mat, preferred_element_type=jnp.float32) + joined_add
        )
        forward_block_len = block_rows.shape[0]
        forward_queries = rotate(
            joined_proj[:, :local_width].reshape(forward_block_len, local_heads, HD), cosv, sinv
        ).astype(jnp.bfloat16)
        forward_keys_rot = rotate(
            joined_proj[:, local_width : 2 * local_width].reshape(
                forward_block_len, local_heads, HD
            ),
            cosv,
            sinv,
        ).astype(jnp.bfloat16)
        forward_values = (
            joined_proj[:, 2 * local_width :]
            .reshape(forward_block_len, local_heads, HD)
            .astype(jnp.bfloat16)
        )
        forward_scores = (
            jnp.einsum(
                "qhd,khd->hqk",
                forward_queries,
                forward_keys_rot,
                preferred_element_type=jnp.float32,
            )
            * score_scale
        )
        forward_scores = jnp.where(allowed_keys(segment)[None], forward_scores, MASKED)
        row_top = jnp.max(forward_scores, axis=2, keepdims=True)
        exponent = jnp.exp(forward_scores - row_top)
        row_total = jnp.sum(exponent, axis=2, keepdims=True)
        forward_log_total = row_top + jnp.log(row_total)
        weights_low = (exponent / row_total).astype(jnp.bfloat16)
        forward_context = jnp.einsum(
            "hqk,khd->qhd", weights_low, forward_values, preferred_element_type=jnp.float32
        )
        forward_context = forward_context.reshape(forward_block_len, local_width).astype(
            jnp.bfloat16
        )
        forward_up_proj = (
            jnp.dot(forward_h_mlp, up_mat, preferred_element_type=jnp.float32) + up_add
        )
        forward_activated = exact_gelu(forward_up_proj).astype(jnp.bfloat16)
        partial_value = jnp.dot(forward_context, dense_mat, preferred_element_type=jnp.float32)
        partial_value = partial_value + jnp.dot(
            forward_activated, down_mat, preferred_element_type=jnp.float32
        )
        branches = lax.psum(partial_value.astype(jnp.bfloat16), "tensor").astype(jnp.float32)
        result = inputs + branches + bias_sum
        forward_stored = (
            forward_normed,
            forward_inv_scale,
            forward_h_attn,
            forward_h_mlp,
            forward_queries,
            forward_keys_rot,
            forward_values,
            forward_log_total,
            forward_context,
            forward_up_proj,
            forward_activated,
        )
        result, stored = (result, forward_stored)
        result_low = result.astype(jnp.bfloat16)
        tick_outputs.append(result_low)
        tick_stored.append((stored, segment, cosv, sinv))
        if section_tick < NMB:
            received = passed_along(result_low, "pipe", 1)
    column_start = lax.axis_index("tensor") * quarter
    section_rows = jnp.concatenate(
        [jnp.where(leading, tick_outputs[block], tick_outputs[block + 1]) for block in range(NMB)],
        axis=0,
    )
    section_out = lax.dynamic_slice_in_dim(section_rows, column_start, quarter, 1)[None]
    returned = jnp.zeros((MB, model_width), jnp.bfloat16)
    tick_grads = []
    totals = None
    for section_tick in range(NMB + 1):
        own_block = min(section_tick, NMB - 1)
        late_tick = max(section_tick - 1, 0)
        upper_tick = min(section_tick + 1, NMB)
        from_output = output_grads[own_block * MB : (own_block + 1) * MB]
        if section_tick == NMB:
            from_output = jnp.zeros_like(from_output)
        grad_rows = jnp.where(leading, returned, from_output)
        stored, segment, cosv, sinv = pick(tick_stored[late_tick], tick_stored[upper_tick])
        (
            normed,
            inv_scale,
            h_attn,
            h_mlp,
            queries,
            keys_rot,
            values,
            log_total,
            context,
            up_proj,
            activated,
        ) = stored
        block_len = grad_rows.shape[0]
        grad_wide = grad_rows.astype(jnp.float32)
        column_sum = jnp.sum(grad_wide, axis=0)
        backward_grad_dense = contract_rows(context, grad_rows)
        backward_grad_down = contract_rows(activated, grad_rows)
        d_context = contract_cols(grad_rows, dense_mat).astype(jnp.bfloat16)
        d_act = contract_cols(grad_rows, down_mat)
        unused, slope_back = jax.vjp(exact_gelu, up_proj)
        d_up = slope_back(d_act)[0].astype(jnp.bfloat16)
        grad_up_add = jnp.sum(d_up.astype(jnp.float32), axis=0)
        backward_grad_up = contract_rows(h_mlp, d_up)
        d_hmlp = contract_cols(d_up, up_mat)
        scores = (
            jnp.einsum("qhd,khd->hqk", queries, keys_rot, preferred_element_type=jnp.float32)
            * score_scale
        )
        scores = jnp.where(allowed_keys(segment)[None], scores, MASKED)
        weights_soft = jnp.exp(scores - log_total)
        d_context3 = d_context.reshape(block_len, local_heads, HD)
        d_values = jnp.einsum(
            "hqk,qhd->khd",
            weights_soft.astype(jnp.bfloat16),
            d_context3,
            preferred_element_type=jnp.float32,
        ).astype(jnp.bfloat16)
        d_weights = jnp.einsum(
            "qhd,khd->hqk", d_context3, values, preferred_element_type=jnp.float32
        )
        row_delta = jnp.sum(weights_soft * d_weights, axis=2, keepdims=True)
        d_scores = (weights_soft * (d_weights - row_delta)).astype(jnp.bfloat16)
        d_queries = (
            jnp.einsum("hqk,khd->qhd", d_scores, keys_rot, preferred_element_type=jnp.float32)
            * score_scale
        )
        d_keys = (
            jnp.einsum("hqk,qhd->khd", d_scores, queries, preferred_element_type=jnp.float32)
            * score_scale
        )
        d_queries = (
            rotate_back(d_queries, cosv, sinv).reshape(block_len, local_width).astype(jnp.bfloat16)
        )
        d_keys = (
            rotate_back(d_keys, cosv, sinv).reshape(block_len, local_width).astype(jnp.bfloat16)
        )
        d_joined = jnp.concatenate(
            [d_queries, d_keys, d_values.reshape(block_len, local_width)], axis=1
        )
        grad_joined_add = jnp.sum(d_joined.astype(jnp.float32), axis=0)
        backward_grad_joined = contract_rows(h_attn, d_joined)
        d_hattn = contract_cols(d_joined, joined_mat)
        d_hattn, d_hmlp = (
            lax.psum(d_hattn.astype(jnp.bfloat16), "tensor").astype(jnp.float32),
            lax.psum(d_hmlp.astype(jnp.bfloat16), "tensor").astype(jnp.float32),
        )
        grad_gains = jnp.concatenate(
            [jnp.sum(d_hattn * normed, axis=0), jnp.sum(d_hmlp * normed, axis=0)]
        )
        grad_shifts = jnp.concatenate([jnp.sum(d_hattn, axis=0), jnp.sum(d_hmlp, axis=0)])
        d_norm = d_hattn * ln_gains[0] + d_hmlp * ln_gains[1]
        grad_input = grad_wide + inv_scale * (
            d_norm
            - jnp.mean(d_norm, axis=1, keepdims=True)
            - normed * jnp.mean(d_norm * normed, axis=1, keepdims=True)
        )
        small_terms = jnp.concatenate(
            [grad_gains, grad_shifts, column_sum, column_sum, grad_joined_add, grad_up_add]
        )
        terms = (
            backward_grad_joined[None],
            backward_grad_dense[None],
            backward_grad_up[None],
            backward_grad_down[None],
            small_terms[None],
        )
        grad_input, terms = (grad_input, terms)
        grad_low = grad_input.astype(jnp.bfloat16)
        tick_grads.append(grad_low)
        if totals is None:
            totals = terms
        else:
            totals = jax.tree.map(lambda older, newer: older + newer, totals, terms)
        if section_tick < NMB:
            returned = passed_along(grad_low, "pipe", -1)
    totals = jax.tree.map(
        lambda part: part.astype(jnp.float32),
        lax.psum_scatter(as_sent(totals), "dp", scatter_dimension=1, tiled=True),
    )
    summed = jax.tree.map(
        lambda part, own: part.astype(own.dtype),
        lax.all_gather(as_sent(totals), "dp", axis=1, tiled=True),
        totals,
    )
    grad_rows_all = jnp.concatenate(
        [jnp.where(leading, tick_grads[block + 1], tick_grads[block]) for block in range(NMB)],
        axis=0,
    )
    input_grad = lax.dynamic_slice_in_dim(grad_rows_all, column_start, quarter, 1)[None]
    grad_joined = summed[0].reshape(1, model_width, 3, local_width)
    grad_dense = summed[1]
    grad_up = summed[2]
    grad_down = summed[3]
    small_sum = summed[4][0]
    offset = 0
    grad_ln_gain = small_sum[offset : offset + 2 * model_width].reshape(1, 2, model_width)
    offset = offset + 2 * model_width
    grad_ln_bias = small_sum[offset : offset + 2 * model_width].reshape(1, 2, model_width)
    offset = offset + 2 * model_width
    grad_output_bias = small_sum[offset : offset + 2 * model_width].reshape(1, 2, model_width)
    offset = offset + 2 * model_width
    grad_joined_bias = small_sum[offset : offset + 3 * local_width].reshape(1, 3, local_width)
    offset = offset + 3 * local_width
    grad_up_bias = small_sum[offset : offset + hidden_local].reshape(1, hidden_local)
    return (
        section_out,
        input_grad,
        grad_ln_gain,
        grad_ln_bias,
        grad_joined,
        grad_joined_bias,
        grad_dense,
        grad_up,
        grad_up_bias,
        grad_down,
        grad_output_bias,
    )


def solution(mesh):
    placed = (
        P("dp", "tensor"),
        P("dp", None),
        P("pipe", None, None),
        P("pipe", None, None),
        P("pipe", None, None, "tensor"),
        P("pipe", None, "tensor"),
        P("pipe", "tensor", None),
        P("pipe", None, "tensor"),
        P("pipe", "tensor"),
        P("pipe", "tensor", None),
        P("pipe", None, None),
        P("dp", "tensor"),
    )
    return jax.shard_map(
        per_device,
        mesh=mesh,
        in_specs=placed,
        out_specs=(
            P("pipe", "dp", "tensor"),
            P("pipe", "dp", "tensor"),
            P("pipe", None, None),
            P("pipe", None, None),
            P("pipe", None, None, "tensor"),
            P("pipe", None, "tensor"),
            P("pipe", "tensor", None),
            P("pipe", None, "tensor"),
            P("pipe", "tensor"),
            P("pipe", "tensor", None),
            P("pipe", None, None),
        ),
        check_vma=False,
    )
```

profile of v0, /device:TPU:1, one launch (start us, length us, event | category | flops | bytes accessed | tf_op | source)
XLA Modules:
  0.0 983.1 jit_solution(12664540825030383722)
XLA Ops:
  11.7 2.6 copy.185
  17.0 21.2 %all-gather.6.cloned.1.call-done = bf16[512,1024]{1,0:T(8,128)(2,1)} async-done(((bf16[512,256]{1,0:T(8,128)(2,1)}), bf16[512,1024]{1,0:T(8,128)(2,1)}) %all-gather.6.cloned.1.call-update) | async-done | bytes 1048592 | tf_op jit(solution)/shard_map/all_gather | solution.py:128
  60.0 32.3 %all-reduce.13.cloned.1.call-done = bf16[128,1024]{1,0:T(8,128)(2,1)} async-done(((bf16[128,1024]{1,0:T(8,128)(2,1)}), bf16[128,1024]{1,0:T(8,128)(2,1)}) %all-reduce.13.cloned.1.call-update) | async-done | bytes 262160 | tf_op jit(solution)/shard_map/psum | solution.py:209
  93.4 5.1 collective-permute-start
  99.2 22.5 %all-gather.8.cloned.1.call-done = bf16[512,1024]{1,0:T(8,128)(2,1)} async-done(((bf16[512,256]{1,0:T(8,128)(2,1)}), bf16[512,1024]{1,0:T(8,128)(2,1)}) %all-gather.8.cloned.1.call-update) | async-done | bytes 1048592 | tf_op jit(solution)/shard_map/all_gather | solution.py:129
  137.5 3.6 convert_reduce_fusion.24
  149.2 42.2 %all-reduce.23.cloned.1.call-done = (bf16[128,1024]{1,0:T(8,128)(2,1)}, bf16[128,1024]{1,0:T(8,128)(2,1)}, bf16[128,1024]{1,0:T(8,128)(2,1)}) async-done(((bf16[128,1024]{1,0:T(8,128)(2,1)}, bf16[128,1024]{1,0:T(8,128)(2,1)}, bf16[128,1024]{1,0:T(8,128)(2,1)}), (bf16[128,1024]{1,0:T(8,128)(2,1)}, bf16[128,1024]{1,0:T(8,128)(2,1)}, bf16[128,1024]{1,0:T(8,128)(2,1)})) %all-reduce.23.cloned.1.call-update) | async-done | bytes 786448 | tf_op jit(solution)/shard_map/psum | solution.py:313
  193.4 4.7 collective-permute-start.1
  198.0 3.9 fusion.386
  210.6 2.9 fusion.53
  237.9 3.5 fusion.395
  242.2 5.4 fusion.377
  247.6 38.0 %all-reduce.21.cloned.1.call-done = (bf16[128,1024]{1,0:T(8,128)(2,1)}, bf16[128,1024]{1,0:T(8,128)(2,1)}, bf16[128,1024]{1,0:T(8,128)(2,1)}) async-done(((bf16[128,1024]{1,0:T(8,128)(2,1)}, bf16[128,1024]{1,0:T(8,128)(2,1)}, bf16[128,1024]{1,0:T(8,128)(2,1)}), (bf16[128,1024]{1,0:T(8,128)(2,1)}, bf16[128,1024]{1,0:T(8,128)(2,1)}, bf16[128,1024]{1,0:T(8,128)(2,1)})) %all-reduce.21.cloned.1.call-update) | async-done | bytes 786448 | tf_op jit(solution)/shard_map/psum | solution.py:313
  287.6 4.5 collective-permute-start.2
  292.2 3.2 collective-permute-done.2
  295.4 3.1 convert_reduce_fusion.11
  308.4 2.9 fusion.56
  332.1 2.5 convert_reduce_fusion.22
  341.1 6.1 fusion.375
  347.2 37.1 %all-reduce.19.cloned.1.call-done = (bf16[128,1024]{1,0:T(8,128)(2,1)}, bf16[128,1024]{1,0:T(8,128)(2,1)}, bf16[128,1024]{1,0:T(8,128)(2,1)}) async-done(((bf16[128,1024]{1,0:T(8,128)(2,1)}, bf16[128,1024]{1,0:T(8,128)(2,1)}, bf16[128,1024]{1,0:T(8,128)(2,1)}), (bf16[128,1024]{1,0:T(8,128)(2,1)}, bf16[128,1024]{1,0:T(8,128)(2,1)}, bf16[128,1024]{1,0:T(8,128)(2,1)})) %all-reduce.19.cloned.1.call-update) | async-done | bytes 786448 | tf_op jit(solution)/shard_map/psum | solution.py:313
  389.2 4.7 collective-permute-start.3
  394.0 2.5 fusion.393
  401.4 3.9 collective-permute-done.6
  423.9 2.5 convert_reduce_fusion.21
  429.9 3.4 fusion.391
  435.3 37.3 %all-reduce.17.cloned.1.call-done = (bf16[128,1024]{1,0:T(8,128)(2,1)}, bf16[128,1024]{1,0:T(8,128)(2,1)}) async-done(((bf16[128,1024]{1,0:T(8,128)(2,1)}, bf16[128,1024]{1,0:T(8,128)(2,1)}), (bf16[128,1024]{1,0:T(8,128)(2,1)}, bf16[128,1024]{1,0:T(8,128)(2,1)})) %all-reduce.17.cloned.1.call-update) | async-done | bytes 524304 | tf_op jit(solution)/shard_map/psum | solution.py:313
  481.0 4.9 collective-permute-done.7
  500.8 5.3 fusion.42
  506.4 4.1 fusion.384
  511.1 2.8 fusion.373
  514.0 2.9 fusion.371
  517.6 4.2 fusion
  542.5 2.6 fusion.41
  551.3 3.0 fusion.46
  554.3 53.3 %reduce-scatter.8.cloned.1.call-done = bf16[1,64,768]{2,1,0:T(8,128)(2,1)} async-done(((bf16[1,1024,768]{2,1,0:T(8,128)(2,1)}), bf16[1,64,768]{2,1,0:T(8,128)(2,1)}) %reduce-scatter.8.cloned.1.call-update) | async-done | bytes 98320 | tf_op jit(solution)/shard_map/reduce_scatter | solution.py:346
  607.7 64.2 %reduce-scatter.14.cloned.1.call-done = bf16[1,64,1024]{2,1,0:T(8,128)(2,1)} async-done(((bf16[1,1024,1024]{2,1,0:T(8,128)(2,1)}), bf16[1,64,1024]{2,1,0:T(8,128)(2,1)}) %reduce-scatter.14.cloned.1.call-update) | async-done | bytes 131088 | tf_op jit(solution)/shard_map/reduce_scatter | solution.py:346
  672.0 64.7 %reduce-scatter.12.cloned.1.call-done = bf16[1,64,1024]{2,1,0:T(8,128)(2,1)} async-done(((bf16[1,1024,1024]{2,1,0:T(8,128)(2,1)}), bf16[1,64,1024]{2,1,0:T(8,128)(2,1)}) %reduce-scatter.12.cloned.1.call-update) | async-done | bytes 131088 | tf_op jit(solution)/shard_map/reduce_scatter | solution.py:346
  740.6 60.6 %reduce-scatter.16.cloned.1.call-done = bf16[496,1]{1,0:T(8,128)(2,1)} async-done(((bf16[7936,1]{1,0:T(8,128)(2,1)}), bf16[496,1]{1,0:T(8,128)(2,1)}) %reduce-scatter.16.cloned.1.call-update) | async-done | bytes 1008
  802.5 53.0 %all-reduce = bf16[7936]{0:T(1024)(128)(2,1)S(1)} all-reduce(bf16[7936]{0:T(1024)(128)(2,1)S(1)} %dynamic-update-slice), channel_id=1, replica_groups=mesh['pipe'=2,'tensor'=4,'dp'=16] {'dp'}, use_global_device_ids=true, to_apply=%add | all-reduce | flops 7936 | bytes 31744
  858.7 4.6 reduce-scatter.10.cloned.1.call-done
  863.3 22.4 %all_gather.25 = bf16[1,256,1024]{2,1,0:T(8,128)(2,1)S(1)} all-gather(bf16[1,16,1024]{2,1,0:T(8,128)(2,1)} %reduce-scatter.10.cloned.1.call-done), channel_id=1, replica_groups=mesh['pipe'=2,'tensor'=4,'dp'=16] {'dp'}, dimensions={1}, use_global_device_ids=true | all-gather | bytes 557056 | tf_op jit(solution)/shard_map/all_gather | solution.py:350
  886.8 14.1 %all-gather.10.cloned.1.call-done = bf16[1,1024,768]{2,1,0:T(8,128)(2,1)} async-done(((bf16[1,64,768]{2,1,0:T(8,128)(2,1)}), bf16[1,1024,768]{2,1,0:T(8,128)(2,1)}) %all-gather.10.cloned.1.call-update) | async-done | bytes 1572880 | tf_op jit(solution)/shard_map/all_gather | solution.py:350
  900.9 3.1 copy.226
  904.0 3.5 copy.227
  907.5 29.0 %all-gather.14.cloned.1.call-done = bf16[1,1024,1024]{2,1,0:T(8,128)(2,1)} async-done(((bf16[1,64,1024]{2,1,0:T(8,128)(2,1)}), bf16[1,1024,1024]{2,1,0:T(8,128)(2,1)}) %all-gather.14.cloned.1.call-update) | async-done | bytes 2097168 | tf_op jit(solution)/shard_map/all_gather | solution.py:350
  936.6 4.1 convert_element_type.728
  940.6 31.6 %all-gather.12.cloned.1.call-done = bf16[1,1024,1024]{2,1,0:T(8,128)(2,1)} async-done(((bf16[1,64,1024]{2,1,0:T(8,128)(2,1)}), bf16[1,1024,1024]{2,1,0:T(8,128)(2,1)}) %all-gather.12.cloned.1.call-update) | async-done | bytes 2097168 | tf_op jit(solution)/shard_map/all_gather | solution.py:350
  972.2 4.1 convert_element_type.725
  (1041 shorter events, 219.6 us)
Async XLA Ops:
  7.2 31.0 %all-gather.6.cloned.1.call-start = ((), (), s32[]{:S(2)}) async-start(), calls=%async_computation.5 | async-start | bytes 1310720 | tf_op jit(solution)/shard_map/all_gather | solution.py:128
  7.9 84.3 %all-reduce.13.cloned.1.call-start = ((), (), s32[]{:S(2)}) async-start(), calls=%async_computation.6 | async-start | bytes 524288 | tf_op jit(solution)/shard_map/psum | solution.py:209
  43.0 90.5 %copy-start.89 = (bf16[128,256]{0,1:T(8,128)(2,1)}, bf16[128,256]{0,1:T(8,128)(2,1)S(1)}, u32[]{:S(2)}) copy-start(bf16[128,256]{0,1:T(8,128)(2,1)S(1)} %copy.186) | copy-start | bytes 196612
  48.4 50.1 %copy-start.335 = (s32[128]{0:T(128)S(1)}, s32[128]{0:T(128)}, u32[]{:S(2)}) copy-start(s32[128]{0:T(128)} %get-tuple-element.267) | copy-start | bytes 1540
  50.6 75.0 %copy-start.126 = (f32[768]{0:T(1024)S(1)}, f32[768]{0:T(1024)}, u32[]{:S(2)}) copy-start(f32[768]{0:T(1024)} %copy-done.125) | copy-start | bytes 9220
  50.6 71.1 %all-gather.8.cloned.1.call-start = ((), (), s32[]{:S(2)}) async-start(), calls=%async_computation.7 | async-start | bytes 1310720 | tf_op jit(solution)/shard_map/all_gather | solution.py:129
  51.3 140.1 %all-reduce.23.cloned.1.call-start = ((), (), s32[]{:S(2)}) async-start(), calls=%async_computation.20 | async-start | bytes 1572864 | tf_op jit(solution)/shard_map/psum | solution.py:313
  53.0 71.2 %copy-start.210 = (f32[128,8]{0,1:T(8,128)}, f32[128,8]{0,1:T(8,128)S(1)}, u32[]{:S(2)}) copy-start(f32[128,8]{0,1:T(8,128)S(1)} %get-tuple-element.115) | copy-start | bytes 12292
  53.6 70.9 %copy-start.211 = (f32[128,8]{0,1:T(8,128)}, f32[128,8]{0,1:T(8,128)S(1)}, u32[]{:S(2)}) copy-start(f32[128,8]{0,1:T(8,128)S(1)} %get-tuple-element.117) | copy-start | bytes 12292
  54.2 70.3 %copy-start.119 = (f32[1,1,1024]{2,1,0:T(1,128)}, f32[1,1,1024]{2,1,0:T(1,128)S(1)}, u32[]{:S(2)}) copy-start(f32[1,1,1024]{2,1,0:T(1,128)S(1)} %convert_add_fusion.10) | copy-start | bytes 12292
  58.2 66.1 %copy-start.212 = (f32[128,8]{0,1:T(8,128)}, f32[128,8]{0,1:T(8,128)S(1)}, u32[]{:S(2)}) copy-start(f32[128,8]{0,1:T(8,128)S(1)} %get-tuple-element.123) | copy-start | bytes 12292
  59.4 65.2 %copy-start.213 = (f32[128,8]{0,1:T(8,128)}, f32[128,8]{0,1:T(8,128)S(1)}, u32[]{:S(2)}) copy-start(f32[128,8]{0,1:T(8,128)S(1)} %get-tuple-element.121) | copy-start | bytes 12292
  59.4 65.2 %copy-start.216 = (f32[128,8]{0,1:T(8,128)}, f32[128,8]{0,1:T(8,128)S(1)}, u32[]{:S(2)}) copy-start(f32[128,8]{0,1:T(8,128)S(1)} %get-tuple-element.231) | copy-start | bytes 12292
  93.4 29.7 %collective-permute-start = (bf16[128,1024]{1,0:T(8,128)(2,1)S(1)}, bf16[128,1024]{1,0:T(8,128)(2,1)S(1)}, u32[]{:S(2)}, u32[]{:S(2)}) collective-permute-start(bf16[128,1024]{1,0:T(8,128)(2,1)S(1)} %fusion.193), channel_id=1, source_target_pairs={{0,64},{1,65},{2,66},{3,67},{4,68},{5,69},{6,70},{7,71},{8,72},{9,... | collective-permute-start | bytes 786440 | tf_op jit(solution)/shard_map/ppermute | solution.py:17
  146.4 139.2 %all-reduce.21.cloned.1.call-start = ((), (), s32[]{:S(2)}) async-start(), calls=%async_computation.19 | async-start | bytes 1572864 | tf_op jit(solution)/shard_map/psum | solution.py:313
  193.4 8.6 collective-permute-start.1
  214.9 9.0 collective-permute-start.4
  237.8 146.5 %all-reduce.19.cloned.1.call-start = ((), (), s32[]{:S(2)}) async-start(), calls=%async_computation.18 | async-start | bytes 1572864 | tf_op jit(solution)/shard_map/psum | solution.py:313
  242.2 53.2 %copy-start.170 = (f32[128]{0:T(128)S(1)}, f32[128]{0:T(128)}, u32[]{:S(2)}) copy-start(f32[128]{0:T(128)} %copy-done.169) | copy-start | bytes 1540
  242.2 53.2 %copy-start.175 = (f32[128]{0:T(128)S(1)}, f32[128]{0:T(128)}, u32[]{:S(2)}) copy-start(f32[128]{0:T(128)} %copy-done.174) | copy-start | bytes 1540
  242.2 53.2 %copy-start.220 = (f32[128]{0:T(128)S(1)}, f32[128]{0:T(128)}, u32[]{:S(2)}) copy-start(f32[128]{0:T(128)} %copy-done.217) | copy-start | bytes 1540
  242.2 53.2 %copy-start.239 = (f32[128]{0:T(128)S(1)}, f32[128]{0:T(128)}, u32[]{:S(2)}) copy-start(f32[128]{0:T(128)} %copy-done.236) | copy-start | bytes 1540
  247.6 51.2 %copy-start.313 = (f32[128]{0:T(128)S(1)}, f32[128]{0:T(128)}, u32[]{:S(2)}) copy-start(f32[128]{0:T(128)} %copy-done.311) | copy-start | bytes 1540
  247.6 51.8 %copy-start.128 = (f32[768]{0:T(1024)S(1)}, f32[768]{0:T(1024)}, u32[]{:S(2)}) copy-start(f32[768]{0:T(1024)} %copy-done.125) | copy-start | bytes 9220
  287.6 7.8 collective-permute-start.2
  312.5 8.9 collective-permute-start.5
  336.9 92.9 %copy-start.70 = (bf16[128,4,64]{0,2,1:T(8,128)(2,1)}, bf16[128,4,64]{0,2,1:T(8,128)(2,1)S(1)}, u32[]{:S(2)}) copy-start(bf16[128,4,64]{0,2,1:T(8,128)(2,1)S(1)} %pad_maximum_fusion.19) | copy-start | bytes 196612
  336.9 92.9 %copy-start.71 = (bf16[128,4,64]{0,2,1:T(8,128)(2,1)}, bf16[128,4,64]{0,2,1:T(8,128)(2,1)S(1)}, u32[]{:S(2)}) copy-start(bf16[128,4,64]{0,2,1:T(8,128)(2,1)S(1)} %pad_maximum_fusion.20) | copy-start | bytes 196612
  338.1 134.5 %all-reduce.17.cloned.1.call-start = ((), (), s32[]{:S(2)}) async-start(), calls=%async_computation.17 | async-start | bytes 1048576 | tf_op jit(solution)/shard_map/psum | solution.py:313
  389.2 9.2 collective-permute-start.3
  396.5 8.7 collective-permute-start.6
  429.8 117.8 %all-reduce.15.cloned.1.call-start = ((), (), s32[]{:S(2)}) async-start(), calls=%async_computation.16 | async-start | bytes 1572864 | tf_op jit(solution)/shard_map/psum | solution.py:313
  477.2 8.8 collective-permute-start.7
  498.7 108.9 %reduce-scatter.8.cloned.1.call-start = ((), (), s32[]{:S(2)}) async-start(), calls=%async_computation.8 | async-start | bytes 1671168 | tf_op jit(solution)/shard_map/reduce_scatter | solution.py:346
  506.1 165.8 %reduce-scatter.14.cloned.1.call-start = ((), (), s32[]{:S(2)}) async-start(), calls=%async_computation.13 | async-start | bytes 2228224 | tf_op jit(solution)/shard_map/reduce_scatter | solution.py:346
  521.9 214.7 %reduce-scatter.12.cloned.1.call-start = ((), (), s32[]{:S(2)}) async-start(), calls=%async_computation.11 | async-start | bytes 2228224 | tf_op jit(solution)/shard_map/reduce_scatter | solution.py:346
  545.3 256.0 %reduce-scatter.16.cloned.1.call-start = ((), (), s32[]{:S(2)}) async-start(), calls=%async_computation.15 | async-start | bytes 2158592
  551.2 312.2 %reduce-scatter.10.cloned.1.call-start = ((), (), s32[]{:S(2)}) async-start(), calls=%async_computation.10 | async-start | bytes 557056 | tf_op jit(solution)/shard_map/reduce_scatter | solution.py:346
  551.2 185.4 %copy-start.343 = (u32[128]{0:T(128)S(1)}, u32[128]{0:T(128)}, u32[]{:S(2)}) copy-start(u32[128]{0:T(128)} %constant.134) | copy-start | bytes 1540
  551.2 186.8 %copy-start.48 = (bf16[128,1024]{1,0:T(8,128)(2,1)S(1)}, bf16[128,1024]{1,0:T(8,128)(2,1)}, u32[]{:S(2)}) copy-start(bf16[128,1024]{1,0:T(8,128)(2,1)} %copy-done.47) | copy-start | bytes 786436
  551.2 186.8 %copy-start.121 = (f32[1,1,1024]{2,1,0:T(1,128)S(1)}, f32[1,1,1024]{2,1,0:T(1,128)}, u32[]{:S(2)}) copy-start(f32[1,1,1024]{2,1,0:T(1,128)} %copy-done.119) | copy-start | bytes 12292
  551.3 186.8 %copy-start.151 = (f32[128]{0:T(128)S(1)}, f32[128]{0:T(128)}, u32[]{:S(2)}) copy-start(f32[128]{0:T(128)} %copy-done.148) | copy-start | bytes 1540
  551.3 186.8 %copy-start.164 = (f32[128]{0:T(128)S(1)}, f32[128]{0:T(128)}, u32[]{:S(2)}) copy-start(f32[128]{0:T(128)} %copy-done.158) | copy-start | bytes 1540
  551.3 186.8 %copy-start.322 = (f32[128]{0:T(128)S(1)}, f32[128]{0:T(128)}, u32[]{:S(2)}) copy-start(f32[128]{0:T(128)} %get-tuple-element.276) | copy-start | bytes 1540
  554.3 185.5 %copy-start.62 = (bf16[128,1024]{1,0:T(8,128)(2,1)S(1)}, bf16[128,1024]{1,0:T(8,128)(2,1)}, u32[]{:S(2)}) copy-start(bf16[128,1024]{1,0:T(8,128)(2,1)} %get-tuple-element.144) | copy-start | bytes 786436
  554.3 346.6 %all-gather.10.cloned.1.call-start = ((), (), s32[]{:S(2)}) async-start(), calls=%async_computation.9 | async-start | bytes 1671168 | tf_op jit(solution)/shard_map/all_gather | solution.py:350
  607.6 328.9 %all-gather.14.cloned.1.call-start = ((), (), s32[]{:S(2)}) async-start(), calls=%async_computation.14 | async-start | bytes 2228224 | tf_op jit(solution)/shard_map/all_gather | solution.py:350
  671.9 300.3 %all-gather.12.cloned.1.call-start = ((), (), s32[]{:S(2)}) async-start(), calls=%async_computation.12 | async-start | bytes 2228224 | tf_op jit(solution)/shard_map/all_gather | solution.py:350
  (326 other events, 1844.2 us)
Sparse Core Ops, SparseCore 0:
  9.7 28.4 all-gather.5
  50.7 41.4 all-reduce.12
  94.0 27.6 all-gather.7
  146.5 44.8 all-reduce.22
  237.9 47.6 all-reduce.20
  338.2 46.0 all-reduce.18
  429.9 42.7 all-reduce.16
  498.8 45.1 all-reduce.14
  546.6 60.9 reduce-scatter.7
  609.8 61.9 reduce-scatter.13
  674.8 61.7 reduce-scatter.11
  739.5 61.7 reduce-scatter.15
  804.2 59.0 reduce-scatter.9
  865.0 35.9 all-gather.9
  902.6 33.9 all-gather.13
  938.2 33.9 all-gather.11
where the time goes:
time: 990 us; the launch traced here: 983 us
  waiting for transfers between devices  568 us (57%)
  matrix products  146 us (15%)
  blocking collectives  75.5 us (8%)
  other arithmetic  75.3 us (8%)
  local copies, waits for them, and re-layouts  71.9 us (7%)
  starting transfers between devices  26.5 us (3%)
  between operations  19.7 us (2%)
    reduce_scatter x4, waiting for transfers between devices, per_device(): lax.psum_scatter(as_sent(totals), 'dp', scatter_dimension=1, tiled=True)  187 us
    psum x5, waiting for transfers between devices, per_device(): lax.psum(d_hmlp.astype(jnp.bfloat16), 'tensor').astype(jnp.float32)  155 us
    all_gather x3, waiting for transfers between devices, per_device(): lax.all_gather(as_sent(totals), 'dp', axis=1, tiled=True)  74.7 us
    unnamed x17, waiting for transfers between devices  62.2 us
    dot_general x20, matrix products, contract_rows(): lax.dot_general(left, right, (((0,), (0,)), ((), ())), preferred_element_...  59.5 us
    unnamed x1, blocking collectives  53 us
    unnamed x742, local copies, waits for them, and re-layouts  32.7 us
    psum x1, waiting for transfers between devices, per_device(): lax.psum(partial_value.astype(jnp.bfloat16), 'tensor').astype(jnp.float32)  32.3 us
  transfers between devices with their start and end apart: 24, of which 19 were waited for; matrix products, arithmetic and copies ran while one was open for 14% of the time, Pallas kernels for 0%

commit v1 on v0

--- a/solution.py
+++ b/solution.py
@@ -1,3 +1,4 @@
+import functools
 import jax
 import jax.numpy as jnp
 from jax import lax
@@ -9,6 +10,14 @@
 NMB = 4
 EPSILON = 1e-05
 MASKED = -1e30
+
+
+def order_the_forms(page, ax_name):
+    ready = jnp.sum(lax.all_gather(page, axis_name=ax_name), axis=0)
+    return ready
+
+
+form_sources_all = functools.partial(order_the_forms, ax_name="tensor")
 
 
 def passed_along(x, axis, by):
@@ -310,7 +319,7 @@
         d_hattn = contract_cols(d_joined, joined_mat)
         d_hattn, d_hmlp = (
             lax.psum(d_hattn.astype(jnp.bfloat16), "tensor").astype(jnp.float32),
-            lax.psum(d_hmlp.astype(jnp.bfloat16), "tensor").astype(jnp.float32),
+            form_sources_all(d_hmlp.astype(jnp.bfloat16)).astype(jnp.float32),
         )
         grad_gains = jnp.concatenate(
             [jnp.sum(d_hattn * normed, axis=0), jnp.sum(d_hmlp * normed, axis=0)]

time: 990 us -> 1090 us (1.10)
  waiting for transfers between devices: 568 us -> 660 us
  other arithmetic: 75.3 us -> 89.1 us
  local copies, waits for them, and re-layouts: 71.9 us -> 59.7 us
    reduce_scatter x4, waiting for transfers between devices: 187 us -> 250 us  [per_device(): lax.psum_scatter(as_sent(totals), 'dp', scatter_dimension=1, tiled=True)]
    all_gather x0 -> x5, waiting for transfers between devices: none -> 57 us  [order_the_forms(): ready = jnp.sum(lax.all_gather(page, axis_name=ax_name), axis=0)]
    all_gather x3, waiting for transfers between devices: 74.7 us -> 40.6 us  [per_device(): lax.all_gather(as_sent(totals), 'dp', axis=1, tiled=True)]
    psum x5, waiting for transfers between devices: 155 us -> 182 us  [per_device(): lax.psum(d_hattn.astype(jnp.bfloat16), 'tensor').astype(jnp.float32)]
    unnamed x17 -> x22, waiting for transfers between devices: 62.2 us -> 40.6 us
    unnamed x742 -> x712, local copies, waits for them, and re-layouts: 32.7 us -> 19.8 us
    dot_general x20, matrix products: 59.5 us -> 48.3 us  [contract_rows(): lax.dot_general(left, right, (((0,), (0,)), ((), ())), preferred_element_...]
  transfers between devices with their start and end apart: 24 -> 29, of which waited for: 19 -> 23; matrix products, arithmetic and copies ran while one was open for 14% -> 15% of each run, Pallas kernels for 0% -> 0%
where the time goes in v1:
time: 1090 us; the launch traced here: 1070 us
  waiting for transfers between devices  660 us (61%)
  matrix products  142 us (13%)
  other arithmetic  89.1 us (8%)
  blocking collectives  75.4 us (7%)
  local copies, waits for them, and re-layouts  59.7 us (5%)
  starting transfers between devices  27.8 us (3%)
  between operations  19.9 us (2%)
    reduce_scatter x4, waiting for transfers between devices, per_device(): lax.psum_scatter(as_sent(totals), 'dp', scatter_dimension=1, tiled=True)  250 us
    psum x5, waiting for transfers between devices, per_device(): lax.psum(d_hattn.astype(jnp.bfloat16), 'tensor').astype(jnp.float32)  182 us
    all_gather x5, waiting for transfers between devices, order_the_forms(): ready = jnp.sum(lax.all_gather(page, axis_name=ax_name), axis=0)  57 us
    unnamed x1, blocking collectives  53 us
    dot_general x20, matrix products, contract_rows(): lax.dot_general(left, right, (((0,), (0,)), ((), ())), preferred_element_...  48.3 us
    unnamed x22, waiting for transfers between devices  40.6 us
    all_gather x3, waiting for transfers between devices, per_device(): lax.all_gather(as_sent(totals), 'dp', axis=1, tiled=True)  40.6 us
    dot_general x20, matrix products, contract_cols(): lax.dot_general(left, right, (((1,), (1,)), ((), ())), preferred_element_...  34.8 us
  transfers between devices with their start and end apart: 29, of which 23 were waited for; matrix products, arithmetic and copies ran while one was open for 15% of the time, Pallas kernels for 0%

profile of v1, /device:TPU:1, one launch (start us, length us, event | category | flops | bytes accessed | tf_op | source)
XLA Modules:
  0.0 1073.7 jit_solution(8525296251708746101)
XLA Ops:
  16.4 21.8 %all-gather.16.cloned.1.call-done = bf16[512,1024]{1,0:T(8,128)(2,1)} async-done(((bf16[512,256]{1,0:T(8,128)(2,1)}), bf16[512,1024]{1,0:T(8,128)(2,1)}) %all-gather.16.cloned.1.call-update) | async-done | bytes 1048592 | tf_op jit(solution)/shard_map/all_gather | solution.py:137
  56.9 34.3 %all-reduce.12.cloned.1.call-done = bf16[128,1024]{1,0:T(8,128)(2,1)} async-done(((bf16[128,1024]{1,0:T(8,128)(2,1)}), bf16[128,1024]{1,0:T(8,128)(2,1)}) %all-reduce.12.cloned.1.call-update) | async-done | bytes 262160 | tf_op jit(solution)/shard_map/psum | solution.py:218
  92.4 4.6 collective-permute-start
  98.4 22.3 %all-gather.18.cloned.1.call-done = bf16[512,1024]{1,0:T(8,128)(2,1)} async-done(((bf16[512,256]{1,0:T(8,128)(2,1)}), bf16[512,1024]{1,0:T(8,128)(2,1)}) %all-gather.18.cloned.1.call-update) | async-done | bytes 1048592 | tf_op jit(solution)/shard_map/all_gather | solution.py:138
  137.8 3.7 convert_reduce_fusion.24
  145.1 35.9 %all-reduce.22.cloned.1.call-done = (bf16[128,1024]{1,0:T(8,128)(2,1)}, bf16[128,1024]{1,0:T(8,128)(2,1)}) async-done(((bf16[128,1024]{1,0:T(8,128)(2,1)}, bf16[128,1024]{1,0:T(8,128)(2,1)}), (bf16[128,1024]{1,0:T(8,128)(2,1)}, bf16[128,1024]{1,0:T(8,128)(2,1)})) %all-reduce.22.cloned.1.call-update) | async-done | bytes 524304 | tf_op jit(solution)/shard_map/psum | solution.py:321
  182.8 5.2 collective-permute-start.1
  190.7 18.1 %all-gather.26.cloned.1.call-done = bf16[512,1024]{1,0:T(8,128)(2,1)} async-done(((bf16[128,1024]{1,0:T(8,128)(2,1)}), bf16[512,1024]{1,0:T(8,128)(2,1)}) %all-gather.26.cloned.1.call-update) | async-done | bytes 1048592 | tf_op jit(solution)/shard_map/all_gather | solution.py:16
  210.4 3.2 convert_reduce_fusion.12
  224.3 2.9 fusion.53
  235.9 3.1 collective-permute-done.4
  249.4 3.7 convert_reduce_fusion.23
  257.5 33.9 %all-reduce.20.cloned.1.call-done = (bf16[128,1024]{1,0:T(8,128)(2,1)}, bf16[128,1024]{1,0:T(8,128)(2,1)}) async-done(((bf16[128,1024]{1,0:T(8,128)(2,1)}, bf16[128,1024]{1,0:T(8,128)(2,1)}), (bf16[128,1024]{1,0:T(8,128)(2,1)}, bf16[128,1024]{1,0:T(8,128)(2,1)})) %all-reduce.20.cloned.1.call-update) | async-done | bytes 524304 | tf_op jit(solution)/shard_map/psum | solution.py:321
  293.3 5.4 collective-permute-start.2
  298.7 6.1 fusion.377
  304.8 14.1 %all-gather.28.cloned.1.call-done = bf16[512,1024]{1,0:T(8,128)(2,1)} async-done(((bf16[128,1024]{1,0:T(8,128)(2,1)}), bf16[512,1024]{1,0:T(8,128)(2,1)}) %all-gather.28.cloned.1.call-update) | async-done | bytes 1048592 | tf_op jit(solution)/shard_map/all_gather | solution.py:16
  321.1 3.3 convert_reduce_fusion.11
  335.1 2.9 fusion.56
  355.7 3.1 fusion.83
  366.1 3.4 fusion.395
  369.6 3.4 fusion.393
  373.0 11.6 %all-gather.30.cloned.1.call-done = bf16[512,1024]{1,0:T(8,128)(2,1)} async-done(((bf16[128,1024]{1,0:T(8,128)(2,1)}), bf16[512,1024]{1,0:T(8,128)(2,1)}) %all-gather.30.cloned.1.call-update) | async-done | bytes 1048592 | tf_op jit(solution)/shard_map/all_gather | solution.py:16
  386.0 43.8 %all-reduce.18.cloned.1.call-done = (bf16[128,1024]{1,0:T(8,128)(2,1)}, bf16[128,1024]{1,0:T(8,128)(2,1)}) async-done(((bf16[128,1024]{1,0:T(8,128)(2,1)}, bf16[128,1024]{1,0:T(8,128)(2,1)}), (bf16[128,1024]{1,0:T(8,128)(2,1)}, bf16[128,1024]{1,0:T(8,128)(2,1)})) %all-reduce.18.cloned.1.call-update) | async-done | bytes 524304 | tf_op jit(solution)/shard_map/psum | solution.py:321
  434.5 4.9 collective-permute-start.3
  480.6 3.4 fusion.92
  484.0 13.2 %all-gather.32.cloned.1.call-done = bf16[512,1024]{1,0:T(8,128)(2,1)} async-done(((bf16[128,1024]{1,0:T(8,128)(2,1)}), bf16[512,1024]{1,0:T(8,128)(2,1)}) %all-gather.32.cloned.1.call-update) | async-done | bytes 1048592 | tf_op jit(solution)/shard_map/all_gather | solution.py:16
  499.4 41.4 %all-reduce.14.cloned.1.call-done = bf16[128,1024]{1,0:T(8,128)(2,1)} async-done(((bf16[128,1024]{1,0:T(8,128)(2,1)}), bf16[128,1024]{1,0:T(8,128)(2,1)}) %all-reduce.14.cloned.1.call-update) | async-done | bytes 262160 | tf_op jit(solution)/shard_map/psum | solution.py:321
  549.1 4.8 collective-permute-done.7
  556.9 3.7 convert_reduce_fusion.20
  568.9 6.8 fusion.42
  576.1 4.1 fusion.375
  580.3 2.8 fusion.373
  583.2 2.9 fusion.371
  586.0 4.2 fusion
  606.4 27.2 %all-reduce.16.cloned.1.call-done = (bf16[128,1024]{1,0:T(8,128)(2,1)}, bf16[128,1024]{1,0:T(8,128)(2,1)}) async-done(((bf16[128,1024]{1,0:T(8,128)(2,1)}, bf16[128,1024]{1,0:T(8,128)(2,1)}), (bf16[128,1024]{1,0:T(8,128)(2,1)}, bf16[128,1024]{1,0:T(8,128)(2,1)})) %all-reduce.16.cloned.1.call-update) | async-done | bytes 524304 | tf_op jit(solution)/shard_map/psum | solution.py:321
  637.7 59.3 %reduce-scatter.8.cloned.1.call-done = bf16[1,64,768]{2,1,0:T(8,128)(2,1)} async-done(((bf16[1,1024,768]{2,1,0:T(8,128)(2,1)}), bf16[1,64,768]{2,1,0:T(8,128)(2,1)}) %reduce-scatter.8.cloned.1.call-update) | async-done | bytes 98320 | tf_op jit(solution)/shard_map/reduce_scatter | solution.py:355
  697.1 64.6 %reduce-scatter.14.cloned.1.call-done = bf16[1,64,1024]{2,1,0:T(8,128)(2,1)} async-done(((bf16[1,1024,1024]{2,1,0:T(8,128)(2,1)}), bf16[1,64,1024]{2,1,0:T(8,128)(2,1)}) %reduce-scatter.14.cloned.1.call-update) | async-done | bytes 131088 | tf_op jit(solution)/shard_map/reduce_scatter | solution.py:355
  761.7 64.8 %reduce-scatter.12.cloned.1.call-done = bf16[1,64,1024]{2,1,0:T(8,128)(2,1)} async-done(((bf16[1,1024,1024]{2,1,0:T(8,128)(2,1)}), bf16[1,64,1024]{2,1,0:T(8,128)(2,1)}) %reduce-scatter.12.cloned.1.call-update) | async-done | bytes 131088 | tf_op jit(solution)/shard_map/reduce_scatter | solution.py:355
  827.8 61.0 %reduce-scatter.10.cloned.1.call-done = bf16[1,16,1024]{2,1,0:T(8,128)(2,1)} async-done(((bf16[1,256,1024]{2,1,0:T(8,128)(2,1)}), bf16[1,16,1024]{2,1,0:T(8,128)(2,1)}) %reduce-scatter.10.cloned.1.call-update) | async-done | bytes 32784 | tf_op jit(solution)/shard_map/reduce_scatter | solution.py:355
  888.8 22.4 %all_gather.65 = bf16[1,256,1024]{2,1,0:T(8,128)(2,1)S(1)} all-gather(bf16[1,16,1024]{2,1,0:T(8,128)(2,1)} %reduce-scatter.10.cloned.1.call-done), channel_id=1, replica_groups=mesh['pipe'=2,'tensor'=4,'dp'=16] {'dp'}, dimensions={1}, use_global_device_ids=true | all-gather | bytes 557056 | tf_op jit(solution)/shard_map/all_gather | solution.py:359
  914.8 38.9 %reduce-scatter.16.cloned.1.call-done = bf16[496,1]{1,0:T(8,128)(2,1)} async-done(((bf16[7936,1]{1,0:T(8,128)(2,1)}), bf16[496,1]{1,0:T(8,128)(2,1)}) %reduce-scatter.16.cloned.1.call-update) | async-done | bytes 1008
  955.0 53.0 %all-reduce = bf16[7936]{0:T(1024)(128)(2,1)S(1)} all-reduce(bf16[7936]{0:T(1024)(128)(2,1)S(1)} %dynamic-update-slice), channel_id=1, replica_groups=mesh['pipe'=2,'tensor'=4,'dp'=16] {'dp'}, use_global_device_ids=true, to_apply=%add | all-reduce | flops 7936 | bytes 31744
  1011.2 3.1 copy.226
  1014.2 3.5 copy.227
  1017.8 9.1 all-gather.24.cloned.1.call-done
  1026.9 4.2 convert_element_type.738
  1031.1 31.5 %all-gather.22.cloned.1.call-done = bf16[1,1024,1024]{2,1,0:T(8,128)(2,1)} async-done(((bf16[1,64,1024]{2,1,0:T(8,128)(2,1)}), bf16[1,1024,1024]{2,1,0:T(8,128)(2,1)}) %all-gather.22.cloned.1.call-update) | async-done | bytes 2097168 | tf_op jit(solution)/shard_map/all_gather | solution.py:359
  1062.5 4.1 convert_element_type.735
  (1031 shorter events, 224.9 us)
Async XLA Ops:
  7.2 31.0 %all-gather.16.cloned.1.call-start = ((), (), s32[]{:S(2)}) async-start(), calls=%async_computation.5 | async-start | bytes 1310720 | tf_op jit(solution)/shard_map/all_gather | solution.py:137
  7.9 83.3 %all-reduce.12.cloned.1.call-start = ((), (), s32[]{:S(2)}) async-start(), calls=%async_computation.6 | async-start | bytes 524288 | tf_op jit(solution)/shard_map/psum | solution.py:218
  43.0 88.1 %copy-start.102 = (bf16[128,256]{0,1:T(8,128)(2,1)}, bf16[128,256]{0,1:T(8,128)(2,1)S(1)}, u32[]{:S(2)}) copy-start(bf16[128,256]{0,1:T(8,128)(2,1)S(1)} %copy.186) | copy-start | bytes 196612
  49.6 71.1 %all-gather.18.cloned.1.call-start = ((), (), s32[]{:S(2)}) async-start(), calls=%async_computation.7 | async-start | bytes 1310720 | tf_op jit(solution)/shard_map/all_gather | solution.py:138
  50.3 130.7 %all-reduce.22.cloned.1.call-start = ((), (), s32[]{:S(2)}) async-start(), calls=%async_computation.25 | async-start | bytes 1048576 | tf_op jit(solution)/shard_map/psum | solution.py:321
  52.1 68.6 %copy-start.205 = (f32[128,8]{0,1:T(8,128)}, f32[128,8]{0,1:T(8,128)S(1)}, u32[]{:S(2)}) copy-start(f32[128,8]{0,1:T(8,128)S(1)} %get-tuple-element.109) | copy-start | bytes 12292
  52.7 68.0 %copy-start.206 = (f32[128,8]{0,1:T(8,128)}, f32[128,8]{0,1:T(8,128)S(1)}, u32[]{:S(2)}) copy-start(f32[128,8]{0,1:T(8,128)S(1)} %get-tuple-element.111) | copy-start | bytes 12292
  53.2 67.5 %copy-start.305 = (s32[128]{0:T(128)}, s32[128]{0:T(128)S(1)}, u32[]{:S(2)}) copy-start(s32[128]{0:T(128)S(1)} %get-tuple-element.119) | copy-start | bytes 1540
  53.2 67.5 %copy-start.124 = (f32[1,1,1024]{2,1,0:T(1,128)}, f32[1,1,1024]{2,1,0:T(1,128)S(1)}, u32[]{:S(2)}) copy-start(f32[1,1,1024]{2,1,0:T(1,128)S(1)} %convert_add_fusion.10) | copy-start | bytes 12292
  55.1 65.6 %copy-start.207 = (f32[128,8]{0,1:T(8,128)}, f32[128,8]{0,1:T(8,128)S(1)}, u32[]{:S(2)}) copy-start(f32[128,8]{0,1:T(8,128)S(1)} %get-tuple-element.117) | copy-start | bytes 12292
  55.1 65.6 %copy-start.209 = (f32[128,8]{0,1:T(8,128)}, f32[128,8]{0,1:T(8,128)S(1)}, u32[]{:S(2)}) copy-start(f32[128,8]{0,1:T(8,128)S(1)} %get-tuple-element.227) | copy-start | bytes 12292
  56.3 64.4 %copy-start.210 = (f32[128,8]{0,1:T(8,128)}, f32[128,8]{0,1:T(8,128)S(1)}, u32[]{:S(2)}) copy-start(f32[128,8]{0,1:T(8,128)S(1)} %get-tuple-element.225) | copy-start | bytes 12292
  92.4 29.7 %collective-permute-start = (bf16[128,1024]{1,0:T(8,128)(2,1)S(1)}, bf16[128,1024]{1,0:T(8,128)(2,1)S(1)}, u32[]{:S(2)}, u32[]{:S(2)}) collective-permute-start(bf16[128,1024]{1,0:T(8,128)(2,1)S(1)} %fusion.193), channel_id=1, source_target_pairs={{0,64},{1,65},{2,66},{3,67},{4,68},{5,69},{6,70},{7,71},{8,72},{9,... | collective-permute-start | bytes 786440 | tf_op jit(solution)/shard_map/ppermute | solution.py:26
  136.6 229.5 %copy-start.65 = (bf16[128,4,64]{0,2,1:T(8,128)(2,1)}, bf16[128,4,64]{0,2,1:T(8,128)(2,1)S(1)}, u32[]{:S(2)}) copy-start(bf16[128,4,64]{0,2,1:T(8,128)(2,1)S(1)} %pad_maximum_fusion.15) | copy-start | bytes 196612
  136.6 229.5 %copy-start.67 = (bf16[128,4,64]{0,2,1:T(8,128)(2,1)}, bf16[128,4,64]{0,2,1:T(8,128)(2,1)S(1)}, u32[]{:S(2)}) copy-start(bf16[128,4,64]{0,2,1:T(8,128)(2,1)S(1)} %pad_maximum_fusion.16) | copy-start | bytes 196612
  137.8 71.1 %all-gather.26.cloned.1.call-start = ((), (), s32[]{:S(2)}) async-start(), calls=%async_computation.16 | async-start | bytes 1310720 | tf_op jit(solution)/shard_map/all_gather | solution.py:16
  143.2 148.2 %all-reduce.20.cloned.1.call-start = ((), (), s32[]{:S(2)}) async-start(), calls=%async_computation.24 | async-start | bytes 1048576 | tf_op jit(solution)/shard_map/psum | solution.py:321
  182.8 27.5 %collective-permute-start.1 = (bf16[128,1024]{1,0:T(8,128)(2,1)S(1)}, bf16[128,1024]{1,0:T(8,128)(2,1)}, u32[]{:S(2)}, u32[]{:S(2)}) collective-permute-start(bf16[128,1024]{1,0:T(8,128)(2,1)S(1)} %get-tuple-element.139), channel_id=1, source_target_pairs={{0,64},{1,65},{2,66},{3,67},{4,68},{5,69},{6,70},{7,71},{8,72},{9,... | collective-permute-start | bytes 786440 | tf_op jit(solution)/shard_map/ppermute | solution.py:26
  229.1 9.9 collective-permute-start.4
  249.3 69.6 %all-gather.28.cloned.1.call-start = ((), (), s32[]{:S(2)}) async-start(), calls=%async_computation.17 | async-start | bytes 1310720 | tf_op jit(solution)/shard_map/all_gather | solution.py:16
  255.4 129.2 %all-gather.30.cloned.1.call-start = ((), (), s32[]{:S(2)}) async-start(), calls=%async_computation.18 | async-start | bytes 1310720 | tf_op jit(solution)/shard_map/all_gather | solution.py:16
  293.3 27.8 %collective-permute-start.2 = (bf16[128,1024]{1,0:T(8,128)(2,1)S(1)}, bf16[128,1024]{1,0:T(8,128)(2,1)}, u32[]{:S(2)}, u32[]{:S(2)}) collective-permute-start(bf16[128,1024]{1,0:T(8,128)(2,1)S(1)} %get-tuple-element.134), channel_id=1, source_target_pairs={{0,64},{1,65},{2,66},{3,67},{4,68},{5,69},{6,70},{7,71},{8,72},{9,... | collective-permute-start | bytes 786440 | tf_op jit(solution)/shard_map/ppermute | solution.py:26
  339.2 10.2 collective-permute-start.5
  358.8 71.0 %all-reduce.18.cloned.1.call-start = ((), (), s32[]{:S(2)}) async-start(), calls=%async_computation.23 | async-start | bytes 1048576 | tf_op jit(solution)/shard_map/psum | solution.py:321
  365.8 131.4 %all-gather.32.cloned.1.call-start = ((), (), s32[]{:S(2)}) async-start(), calls=%async_computation.19 | async-start | bytes 1310720 | tf_op jit(solution)/shard_map/all_gather | solution.py:16
  434.5 8.8 collective-permute-start.3
  441.8 8.7 collective-permute-start.6
  471.8 68.9 %all-reduce.14.cloned.1.call-start = ((), (), s32[]{:S(2)}) async-start(), calls=%async_computation.8 | async-start | bytes 524288 | tf_op jit(solution)/shard_map/psum | solution.py:321
  474.8 71.8 %copy-start.81 = (bf16[128,4,64]{0,2,1:T(8,128)(2,1)}, bf16[128,4,64]{0,2,1:T(8,128)(2,1)S(1)}, u32[]{:S(2)}) copy-start(bf16[128,4,64]{0,2,1:T(8,128)(2,1)S(1)} %pad_maximum_fusion.21) | copy-start | bytes 196612
  474.8 71.8 %copy-start.83 = (bf16[128,4,64]{0,2,1:T(8,128)(2,1)}, bf16[128,4,64]{0,2,1:T(8,128)(2,1)S(1)}, u32[]{:S(2)}) copy-start(bf16[128,4,64]{0,2,1:T(8,128)(2,1)S(1)} %pad_maximum_fusion.22) | copy-start | bytes 196612
  480.1 124.8 %all-gather.34.cloned.1.call-start = ((), (), s32[]{:S(2)}) async-start(), calls=%async_computation.20 | async-start | bytes 1310720 | tf_op jit(solution)/shard_map/all_gather | solution.py:16
  545.2 8.7 collective-permute-start.7
  563.0 70.6 %all-reduce.16.cloned.1.call-start = ((), (), s32[]{:S(2)}) async-start(), calls=%async_computation.22 | async-start | bytes 1048576 | tf_op jit(solution)/shard_map/psum | solution.py:321
  568.9 128.1 %reduce-scatter.8.cloned.1.call-start = ((), (), s32[]{:S(2)}) async-start(), calls=%async_computation.9 | async-start | bytes 1671168 | tf_op jit(solution)/shard_map/reduce_scatter | solution.py:355
  575.8 185.8 %reduce-scatter.14.cloned.1.call-start = ((), (), s32[]{:S(2)}) async-start(), calls=%async_computation.14 | async-start | bytes 2228224 | tf_op jit(solution)/shard_map/reduce_scatter | solution.py:355
  590.3 236.1 %reduce-scatter.12.cloned.1.call-start = ((), (), s32[]{:S(2)}) async-start(), calls=%async_computation.12 | async-start | bytes 2228224 | tf_op jit(solution)/shard_map/reduce_scatter | solution.py:355
  599.5 289.2 %reduce-scatter.10.cloned.1.call-start = ((), (), s32[]{:S(2)}) async-start(), calls=%async_computation.11 | async-start | bytes 557056 | tf_op jit(solution)/shard_map/reduce_scatter | solution.py:355
  604.8 349.0 %reduce-scatter.16.cloned.1.call-start = ((), (), s32[]{:S(2)}) async-start(), calls=%async_computation.21 | async-start | bytes 2158592
  635.7 190.8 %copy-start.332 = (u32[128]{0:T(128)S(1)}, u32[128]{0:T(128)}, u32[]{:S(2)}) copy-start(u32[128]{0:T(128)} %constant.139) | copy-start | bytes 1540
  637.6 274.7 %copy-start.327 = (f32[128]{0:T(128)S(1)}, f32[128]{0:T(128)}, u32[]{:S(2)}) copy-start(f32[128]{0:T(128)} %get-tuple-element.62) | copy-start | bytes 1540
  637.6 274.7 %copy-start.326 = (f32[128]{0:T(128)S(1)}, f32[128]{0:T(128)}, u32[]{:S(2)}) copy-start(f32[128]{0:T(128)} %get-tuple-element.72) | copy-start | bytes 1540
  637.6 274.7 %copy-start.43 = (bf16[128,1024]{1,0:T(8,128)(2,1)S(1)}, bf16[128,1024]{1,0:T(8,128)(2,1)}, u32[]{:S(2)}) copy-start(bf16[128,1024]{1,0:T(8,128)(2,1)} %copy-done.42) | copy-start | bytes 786436
  637.6 274.7 %copy-start.48 = (bf16[128,1024]{1,0:T(8,128)(2,1)S(1)}, bf16[128,1024]{1,0:T(8,128)(2,1)}, u32[]{:S(2)}) copy-start(bf16[128,1024]{1,0:T(8,128)(2,1)} %get-tuple-element.88) | copy-start | bytes 786436
  637.6 274.8 %copy-start.126 = (f32[1,1,1024]{2,1,0:T(1,128)S(1)}, f32[1,1,1024]{2,1,0:T(1,128)}, u32[]{:S(2)}) copy-start(f32[1,1,1024]{2,1,0:T(1,128)} %copy-done.124) | copy-start | bytes 12292
  637.6 274.8 %copy-start.312 = (f32[128]{0:T(128)S(1)}, f32[128]{0:T(128)}, u32[]{:S(2)}) copy-start(f32[128]{0:T(128)} %get-tuple-element.270) | copy-start | bytes 1540
  637.6 373.5 %all-gather.20.cloned.1.call-start = ((), (), s32[]{:S(2)}) async-start(), calls=%async_computation.10 | async-start | bytes 1671168 | tf_op jit(solution)/shard_map/all_gather | solution.py:359
  697.0 329.8 %all-gather.24.cloned.1.call-start = ((), (), s32[]{:S(2)}) async-start(), calls=%async_computation.15 | async-start | bytes 2228224 | tf_op jit(solution)/shard_map/all_gather | solution.py:359
  761.6 300.9 %all-gather.22.cloned.1.call-start = ((), (), s32[]{:S(2)}) async-start(), calls=%async_computation.13 | async-start | bytes 2228224 | tf_op jit(solution)/shard_map/all_gather | solution.py:359
  (316 other events, 1972.4 us)
Sparse Core Ops, SparseCore 0:
  9.7 28.4 all-gather.15
  49.7 41.4 all-reduce.11
  93.0 27.6 all-gather.17
  137.9 43.0 all-reduce.21
  183.2 25.6 all-gather.25
  249.5 41.9 all-reduce.19
  293.2 25.6 all-gather.27
  358.9 25.6 all-gather.29
  387.1 42.6 all-reduce.17
  471.9 25.1 all-gather.31
  499.6 41.0 all-reduce.13
  563.1 25.3 all-gather.33
  590.9 42.6 all-reduce.15
  635.8 61.1 reduce-scatter.7
  699.9 61.6 reduce-scatter.13
  764.6 61.8 reduce-scatter.11
  829.4 59.3 reduce-scatter.9
  891.6 62.1 reduce-scatter.15
  955.4 35.5 all-gather.19
  992.6 34.1 all-gather.23
  1028.6 33.9 all-gather.21
